TPU v7x, 32 devices: a whole 2x2x4 slice. The times are simulated.
32 devices in a mesh: seq: 8 (over z, core), head: 4 (over y, x).
Axes of the slice: x: 2, y: 2, z: 4, core: 2. Of those that a mesh axis runs over, the one named last changes fastest.
Arguments:
- video_query: bfloat16 [4096, 3072], P(('seq', 'head')), may hold values from -8 to 8
- video_key: bfloat16 [4096, 3072], P(('seq', 'head')), may hold values from -8 to 8
- video_value: bfloat16 [4096, 3072], P(('seq', 'head')), may hold values from -6 to 6
- video_grad: bfloat16 [4096, 3072], P(('seq', 'head')), may hold values from -6 to 6
- text_query: bfloat16 [256, 3072], P(None, 'head'), may hold values from -8 to 8
- text_key: bfloat16 [256, 3072], P(None, 'head'), may hold values from -8 to 8
- text_value: bfloat16 [256, 3072], P(None, 'head'), may hold values from -6 to 6
- text_grad: bfloat16 [256, 3072], P(None, 'head'), may hold values from -6 to 6
- tile_list: int32 [32, 8], replicated, may hold values from 0 to 31, as said below
- tile_count: int32 [32], replicated, may hold values from 1 to 8, as said below
- text_mask: int32 [256], replicated, may hold values from 0 to 1, as said below
Outputs:
- attended_video: bfloat16 [4096, 3072], P(('seq', 'head'))
- video_query_grad: bfloat16 [4096, 3072], P(('seq', 'head'))
- video_key_grad: bfloat16 [4096, 3072], P(('seq', 'head'))
- video_value_grad: bfloat16 [4096, 3072], P(('seq', 'head'))
- attended_text: bfloat16 [256, 3072], P(None, 'head')
- text_query_grad: bfloat16 [256, 3072], P(None, 'head')
- text_key_grad: bfloat16 [256, 3072], P(None, 'head')
- text_value_grad: bfloat16 [256, 3072], P(None, 'head')
Inputs may be any that keep to these rules, and one draw needn't show every extreme that they name: `tile_list`: the 8 entries of one query tile's list are distinct. Query tiles fall in aligned blocks of 4; the used entries of one block together name at most 2 distinct tiles of any other block of 4 tiles, and every block names exactly 2 from some other block. `tile_count`: every aligned block of 4 query tiles has a tile that uses all 8 entries. `text_mask`: the ones form a prefix of at least 64 entries.
All inputs are finite; a program needn't handle non-finite values.
Results may differ from a plain program's by a relative error of at most 0.012.
Values may be sent and summed in bfloat16 or wider, within the bound.
A program may use at most 192 MiB of HBM per device.

v0:
```python
import jax
import jax.numpy as jnp
from jax import lax
from jax.sharding import PartitionSpec as P

HD = 128
TXT = 256
TILE = 128
KT = 8
MOST = 2
NEGATIVE = -1e30
HIGHEST_PRECISION = lax.Precision.HIGHEST


def split_product(form, weights, data):
    upper = weights.astype(jnp.bfloat16)
    lower = (weights - upper.astype(jnp.float32)).astype(jnp.bfloat16)
    return jnp.einsum(form, upper, data, preferred_element_type=jnp.float32) + jnp.einsum(
        form, lower, data, preferred_element_type=jnp.float32
    )


def block_scores(query_blk, key_blk, live_blk, factor):
    scores = (
        jnp.einsum("bthd,bkhd->bhtk", query_blk, key_blk, preferred_element_type=jnp.float32)
        * factor
    )
    scores = jnp.where(live_blk[:, None, None, :], scores, NEGATIVE)
    maximum = jnp.max(scores, axis=-1)
    log_total = maximum + jnp.log(jnp.sum(jnp.exp(scores - maximum[..., None]), axis=-1))
    return (scores, log_total)


def block_forward(scores, log_total, value_blk, grad_blk):
    weights = jnp.exp(scores - log_total[..., None]).astype(jnp.bfloat16)
    output = jnp.einsum("bhtk,bkhd->bthd", weights, value_blk, preferred_element_type=jnp.float32)
    offset = jnp.sum(grad_blk.astype(jnp.float32) * output, axis=-1)
    return (output, jnp.transpose(offset, (0, 2, 1)))


def block_backward(scores, log_total, offset, query_blk, key_blk, value_blk, grad_blk, factor):
    probability = jnp.exp(scores - log_total[..., None])
    weights = probability.astype(jnp.bfloat16)
    prob_grad = jnp.einsum(
        "bthd,bkhd->bhtk", grad_blk, value_blk, preferred_element_type=jnp.float32
    )
    score_grad = (probability * (prob_grad - offset[..., None])).astype(jnp.bfloat16)
    query_grad = (
        jnp.einsum("bhtk,bkhd->bthd", score_grad, key_blk, preferred_element_type=jnp.float32)
        * factor
    )
    key_grad = (
        jnp.einsum("bhtk,bthd->bkhd", score_grad, query_blk, preferred_element_type=jnp.float32)
        * factor
    )
    value_grad = jnp.einsum(
        "bhtk,bthd->bkhd", weights, grad_blk, preferred_element_type=jnp.float32
    )
    return (query_grad, key_grad, value_grad)


def spread_grads(pool_total, text_total, grad_blk, pool_slot):
    block_tiles = grad_blk.shape[0]
    tile_part = grad_blk[:, : KT * TILE].reshape(block_tiles, KT, TILE, pool_total.shape[2])
    return (
        pool_total.at[pool_slot].add(tile_part),
        text_total + jnp.sum(grad_blk[:, KT * TILE :], axis=0),
    )


def body(
    video_query,
    video_key,
    video_value,
    video_grad,
    text_query,
    text_key,
    text_value,
    text_grad,
    tile_list,
    tile_count,
    text_mask,
):
    factor = HD ** (-0.5)
    groups = lax.axis_size("seq")
    own_group = lax.axis_index("seq")
    query_rows, key_rows, value_rows, grad_rows = (
        lax.all_to_all(video_query, "head", split_axis=1, concat_axis=0, tiled=True),
        lax.all_to_all(video_key, "head", split_axis=1, concat_axis=0, tiled=True),
        lax.all_to_all(video_value, "head", split_axis=1, concat_axis=0, tiled=True),
        lax.all_to_all(video_grad, "head", split_axis=1, concat_axis=0, tiled=True),
    )
    token_rows, feature_width = query_rows.shape
    head_count = feature_width // HD
    shard_tiles = token_rows // TILE
    tile_total = tile_list.shape[0]
    text_ok = text_mask > 0
    entry_live = jnp.arange(KT)[None, :] < tile_count[:, None]
    tile_hits = (tile_list[:, :, None] == jnp.arange(tile_total)[None, None, :]) & entry_live[
        :, :, None
    ]
    wanted = jnp.any(
        jnp.any(tile_hits, axis=1).reshape(groups, shard_tiles, tile_total), axis=1
    ).reshape(groups, groups, shard_tiles)
    slot_rank = jnp.cumsum(wanted.astype(jnp.int32), axis=2) - 1
    distinct = (jnp.arange(groups)[:, None] != jnp.arange(groups)[None, :])[:, :, None, None]
    select = (
        wanted[:, :, None, :]
        & (slot_rank[:, :, None, :] == jnp.arange(MOST)[None, None, :, None])
        & distinct
    )
    outgoing = lax.dynamic_index_in_dim(select, own_group, 1, keepdims=False)
    incoming = lax.dynamic_index_in_dim(select, own_group, 0, keepdims=False)
    picker = outgoing.reshape(groups * MOST, shard_tiles).astype(jnp.bfloat16)
    send_keys = jnp.dot(
        picker,
        key_rows.reshape(shard_tiles, TILE * feature_width),
        preferred_element_type=jnp.float32,
    )
    send_keys = send_keys.astype(jnp.bfloat16).reshape(groups, MOST * TILE, feature_width)
    send_values = jnp.dot(
        picker,
        value_rows.reshape(shard_tiles, TILE * feature_width),
        preferred_element_type=jnp.float32,
    )
    send_values = send_values.astype(jnp.bfloat16).reshape(groups, MOST * TILE, feature_width)
    owner_base = (
        jnp.arange(groups, dtype=jnp.int32)[:, None, None] * shard_tiles
        + jnp.arange(shard_tiles, dtype=jnp.int32)[None, None, :]
    )
    slot_ids = jnp.where(
        jnp.any(incoming, axis=2), jnp.sum(jnp.where(incoming, owner_base, 0), axis=2), -1
    ).reshape(groups * MOST)
    pool_ids = jnp.concatenate(
        [own_group * shard_tiles + jnp.arange(shard_tiles, dtype=jnp.int32), slot_ids]
    )
    pool_size = shard_tiles + groups * MOST
    my_list = lax.dynamic_slice_in_dim(tile_list, own_group * shard_tiles, shard_tiles, 0)
    my_count = lax.dynamic_slice_in_dim(tile_count, own_group * shard_tiles, shard_tiles, 0)
    pool_match = my_list[:, :, None] == pool_ids[None, None, :]
    pool_slot = jnp.sum(jnp.where(pool_match, jnp.arange(pool_size, dtype=jnp.int32), 0), axis=2)
    live_entry = jnp.any(pool_match, axis=2) & (jnp.arange(KT)[None, :] < my_count[:, None])
    text_query3 = text_query.reshape(TXT, head_count, HD)
    text_key3 = text_key.reshape(TXT, head_count, HD)
    text_value3 = text_value.reshape(TXT, head_count, HD)
    text_grad3 = text_grad.reshape(TXT, head_count, HD)
    block_tiles = min(shard_tiles, max(1, 512 // TILE))
    block_count = shard_tiles // block_tiles
    query_blocks = query_rows.reshape(block_count, block_tiles, TILE, head_count, HD)
    grad_blocks = grad_rows.reshape(block_count, block_tiles, TILE, head_count, HD)
    slot_blocks = pool_slot.reshape(block_count, block_tiles, KT)
    live_blocks = jnp.concatenate(
        [
            jnp.repeat(live_entry, TILE, axis=1),
            jnp.broadcast_to(text_ok[None, :], (shard_tiles, TXT)),
        ],
        axis=1,
    )
    live_blocks = live_blocks.reshape(block_count, block_tiles, KT * TILE + TXT)
    local_keys = key_rows.reshape(shard_tiles, TILE, feature_width)
    local_values = value_rows.reshape(shard_tiles, TILE, feature_width)

    def build_pool(received):
        got_keys, got_values = received
        return (
            jnp.concatenate(
                [local_keys, got_keys.reshape(groups * MOST, TILE, feature_width)], axis=0
            ),
            jnp.concatenate(
                [local_values, got_values.reshape(groups * MOST, TILE, feature_width)], axis=0
            ),
        )

    def block_rows(pool, slot_blk, text_part):
        picked = pool[slot_blk].reshape(block_tiles, KT * TILE, head_count, HD)
        return jnp.concatenate(
            [picked, jnp.broadcast_to(text_part[None], (block_tiles, TXT, head_count, HD))], axis=1
        )

    pool_keys, pool_values = build_pool(
        (
            lax.all_to_all(send_keys, "seq", split_axis=0, concat_axis=0, tiled=True),
            lax.all_to_all(send_values, "seq", split_axis=0, concat_axis=0, tiled=True),
        )
    )
    start = (
        jnp.zeros((pool_size, TILE, feature_width), jnp.float32),
        jnp.zeros((pool_size, TILE, feature_width), jnp.float32),
        jnp.zeros((TXT, head_count, HD), jnp.float32),
        jnp.zeros((TXT, head_count, HD), jnp.float32),
    )

    def forward_step(running, inputs):
        query_blk, grad_blk, slot_blk, live_blk = inputs
        key_blk = block_rows(pool_keys, slot_blk, text_key3)
        value_blk = block_rows(pool_values, slot_blk, text_value3)
        scores, log_total = block_scores(query_blk, key_blk, live_blk, factor)
        output, offset = block_forward(scores, log_total, value_blk, grad_blk)
        return (running, (output.astype(jnp.bfloat16), log_total, offset))

    unused, forwards = lax.scan(
        forward_step, None, (query_blocks, grad_blocks, slot_blocks, live_blocks)
    )
    attended_blocks, total_blocks, offset_blocks = forwards
    again_keys, again_values = build_pool(
        (
            lax.all_to_all(send_keys, "seq", split_axis=0, concat_axis=0, tiled=True),
            lax.all_to_all(send_values, "seq", split_axis=0, concat_axis=0, tiled=True),
        )
    )

    def backward_step(running, inputs):
        key_acc, value_acc, text_key_acc, text_value_acc = running
        query_blk, grad_blk, slot_blk, live_blk, log_total, offset = inputs
        key_blk = block_rows(again_keys, slot_blk, text_key3)
        value_blk = block_rows(again_values, slot_blk, text_value3)
        scores, unused_total = block_scores(query_blk, key_blk, live_blk, factor)
        query_grad, key_grad, value_grad = block_backward(
            scores, log_total, offset, query_blk, key_blk, value_blk, grad_blk, factor
        )
        key_acc, text_key_acc = spread_grads(key_acc, text_key_acc, key_grad, slot_blk)
        value_acc, text_value_acc = spread_grads(value_acc, text_value_acc, value_grad, slot_blk)
        return ((key_acc, value_acc, text_key_acc, text_value_acc), query_grad.astype(jnp.bfloat16))

    finals, query_grad_blocks = lax.scan(
        backward_step,
        start,
        (query_blocks, grad_blocks, slot_blocks, live_blocks, total_blocks, offset_blocks),
    )
    key_acc, value_acc, text_key_acc, text_value_acc = finals
    back_keys, back_values = (
        lax.all_to_all(
            key_acc[shard_tiles:].reshape(groups, MOST * TILE, feature_width),
            "seq",
            split_axis=0,
            concat_axis=0,
            tiled=True,
        ),
        lax.all_to_all(
            value_acc[shard_tiles:].reshape(groups, MOST * TILE, feature_width),
            "seq",
            split_axis=0,
            concat_axis=0,
            tiled=True,
        ),
    )
    out_flat = outgoing.reshape(groups * MOST, shard_tiles)
    target_tile = jnp.where(
        jnp.any(out_flat, axis=1),
        jnp.sum(jnp.where(out_flat, jnp.arange(shard_tiles, dtype=jnp.int32)[None, :], 0), axis=1),
        shard_tiles,
    )
    own_key_grad = (
        key_acc[:shard_tiles]
        .at[target_tile]
        .add(back_keys.reshape(groups * MOST, TILE, feature_width), mode="drop")
    )
    own_value_grad = (
        value_acc[:shard_tiles]
        .at[target_tile]
        .add(back_values.reshape(groups * MOST, TILE, feature_width), mode="drop")
    )
    key_rows3 = key_rows.reshape(token_rows, head_count, HD)
    value_rows3 = value_rows.reshape(token_rows, head_count, HD)
    text_query32 = text_query3.astype(jnp.float32)
    text_key32 = text_key3.astype(jnp.float32)
    text_value32 = text_value3.astype(jnp.float32)
    text_grad32 = text_grad3.astype(jnp.float32)
    video_scores = (
        jnp.einsum("thd,khd->htk", text_query3, key_rows3, preferred_element_type=jnp.float32)
        * factor
    )
    text_scores = (
        jnp.einsum("thd,khd->htk", text_query3, text_key3, preferred_element_type=jnp.float32)
        * factor
    )
    text_scores = jnp.where(text_ok[None, None, :], text_scores, NEGATIVE)
    maximum = jnp.maximum(
        lax.pmax(jnp.max(video_scores, axis=-1), "seq"), jnp.max(text_scores, axis=-1)
    )
    video_exp = jnp.exp(video_scores - maximum[..., None])
    denominator, numerator = lax.psum(
        (jnp.sum(video_exp, axis=-1), split_product("htk,khd->thd", video_exp, value_rows3)), "seq"
    )
    text_exp = jnp.exp(text_scores - maximum[..., None])
    denominator = denominator + jnp.sum(text_exp, axis=-1)
    numerator = numerator + jnp.einsum(
        "htk,khd->thd", text_exp, text_value32, precision=HIGHEST_PRECISION
    )
    log_total = maximum + jnp.log(denominator)
    text_out = numerator / denominator.T[:, :, None]
    video_prob = jnp.exp(video_scores - log_total[..., None])
    text_prob = jnp.exp(text_scores - log_total[..., None])
    text_offset = jnp.sum(text_grad32 * text_out, axis=-1).T
    video_dscore = video_prob * (
        jnp.einsum("thd,khd->htk", text_grad3, value_rows3, preferred_element_type=jnp.float32)
        - text_offset[..., None]
    )
    text_dscore = text_prob * (
        jnp.einsum("thd,khd->htk", text_grad3, text_value3, preferred_element_type=jnp.float32)
        - text_offset[..., None]
    )
    query_part = split_product("htk,khd->thd", video_dscore, key_rows3) * factor
    video_key_from_text = split_product("htk,thd->khd", video_dscore, text_query3) * factor
    video_value_from_text = split_product("htk,thd->khd", video_prob, text_grad3)
    query_sum, key_sum, value_sum = lax.psum((query_part, text_key_acc, text_value_acc), "seq")
    text_query_grad = (
        query_sum
        + jnp.einsum("htk,khd->thd", text_dscore, text_key32, precision=HIGHEST_PRECISION) * factor
    )
    text_key_grad = (
        key_sum
        + jnp.einsum("htk,thd->khd", text_dscore, text_query32, precision=HIGHEST_PRECISION)
        * factor
    )
    text_value_grad = value_sum + jnp.einsum(
        "htk,thd->khd", text_prob, text_grad32, precision=HIGHEST_PRECISION
    )
    attended_rows = attended_blocks.reshape(token_rows, feature_width)
    query_grad_rows = query_grad_blocks.reshape(token_rows, feature_width)
    key_grad_rows = (
        own_key_grad.reshape(token_rows, feature_width)
        + video_key_from_text.reshape(token_rows, feature_width)
    ).astype(jnp.bfloat16)
    value_grad_rows = (
        own_value_grad.reshape(token_rows, feature_width)
        + video_value_from_text.reshape(token_rows, feature_width)
    ).astype(jnp.bfloat16)
    attended_video, video_query_grad, video_key_grad, video_value_grad = (
        lax.all_to_all(attended_rows, "head", split_axis=0, concat_axis=1, tiled=True),
        lax.all_to_all(query_grad_rows, "head", split_axis=0, concat_axis=1, tiled=True),
        lax.all_to_all(key_grad_rows, "head", split_axis=0, concat_axis=1, tiled=True),
        lax.all_to_all(value_grad_rows, "head", split_axis=0, concat_axis=1, tiled=True),
    )
    return (
        attended_video,
        video_query_grad,
        video_key_grad,
        video_value_grad,
        text_out.reshape(TXT, feature_width).astype(jnp.bfloat16),
        text_query_grad.reshape(TXT, feature_width).astype(jnp.bfloat16),
        text_key_grad.reshape(TXT, feature_width).astype(jnp.bfloat16),
        text_value_grad.reshape(TXT, feature_width).astype(jnp.bfloat16),
    )


def solution(mesh):
    placed = (
        P(("seq", "head"), None),
        P(("seq", "head"), None),
        P(("seq", "head"), None),
        P(("seq", "head"), None),
        P(None, "head"),
        P(None, "head"),
        P(None, "head"),
        P(None, "head"),
        P(),
        P(),
        P(),
    )
    return jax.shard_map(
        body,
        mesh=mesh,
        in_specs=placed,
        out_specs=(
            P(("seq", "head"), None),
            P(("seq", "head"), None),
            P(("seq", "head"), None),
            P(("seq", "head"), None),
            P(None, "head"),
            P(None, "head"),
            P(None, "head"),
            P(None, "head"),
        ),
        check_vma=False,
    )
```

profile of v0, /device:TPU:0, one launch (start us, length us, event | category | flops | bytes accessed | tf_op | source)
XLA Modules:
  0.0 900.4 jit_solution(9937720170638479781)
XLA Ops:
  17.2 8.8 all-to-all-done
  50.8 66.3 %all-to-all-done.1 = bf16[8,256,768]{2,1,0:T(8,128)(2,1)} async-done(((bf16[8,256,768]{2,1,0:T(8,128)(2,1)}), bf16[8,256,768]{2,1,0:T(8,128)(2,1)}, u32[]{:S(2)}, u32[]{:S(2)}) %all-to-all-start.1) | async-done | bytes 3145760 | tf_op jit(solution)/shard_map/all_to_all | solution.py:183
  124.7 67.4 %all-to-all-done.3 = bf16[8,256,768]{2,1,0:T(8,128)(2,1)S(1)} async-done(((bf16[8,256,768]{2,1,0:T(8,128)(2,1)}), bf16[8,256,768]{2,1,0:T(8,128)(2,1)S(1)}, u32[]{:S(2)}, u32[]{:S(2)}) %all-to-all-start.3) | async-done | bytes 3145760 | tf_op jit(solution)/shard_map/all_to_all | solution.py:182
  206.3 5.8 gather_fusion.1
  212.1 13.7 %reshape.401 = bf16[4,1024,6,128]{3,2,1,0:T(8,128)(2,1)} reshape(bf16[32,128,768]{2,1,0:T(8,128)(2,1)} %gather_fusion.1) | data formatting | bytes 12582912 | tf_op jit(solution)/shard_map/while/body/eval_jaxpr/reshape | solution.py:175
  225.8 7.5 copy.386
  237.3 5.8 gather_fusion
  243.1 13.7 %reshape.400 = bf16[4,1024,6,128]{3,2,1,0:T(8,128)(2,1)} reshape(bf16[32,128,768]{2,1,0:T(8,128)(2,1)} %gather_fusion) | data formatting | bytes 12582912 | tf_op jit(solution)/shard_map/while/body/eval_jaxpr/reshape | solution.py:175
  256.8 11.5 %copy.380 = bf16[4,1024,6,128]{1,3,2,0:T(8,128)(2,1)} copy(bf16[4,1024,6,128]{3,2,1,0:T(8,128)(2,1)} %reshape.400) | data formatting | bytes 12582912 | tf_op jit(solution)/shard_map/while/body/eval_jaxpr/reshape | solution.py:175
  272.8 5.9 bitcast_reduce_fusion
  285.6 10.6 %bitcast_convert_fusion = (bf16[4,128,6,128]{1,3,2,0:T(8,128)(2,1)}, f32[4,6,128,128]{3,2,1,0:T(8,128)S(1)}) fusion(f32[4,6,1280,128]{3,2,1,0:T(8,128)} %copy-done.2, f32[4,6,128]{2,1,0:T(8,128)S(1)} %log_add_fusion, pred[4,1280]{1,0:T(4,128)(4,1)S(1)} %pad_add_fusion, bf16[4,256,6,128]{1,3,2,0:T(8,128)(2,1)S(1)} %broadcast_in_dim.182, ...), kind=kOutput, calls=%fused_computation.44 | convolution fusion | flops 1038483456 | bytes 25969664 | tf_op jit(solution)/shard_map/while/body/eval_jaxpr/bhtk,bkhd->bthd/dot_general | solution.py:36
  300.9 13.0 %fusion = bf16[4,6,128,1280]{2,3,1,0:T(8,128)(2,1)} fusion(f32[4,6,1280,128]{3,2,1,0:T(8,128)} %copy-done.2, bf16[4,128,6,128]{1,3,2,0:T(8,128)(2,1)S(1)} %bitcast.180, f32[4,6,128]{2,1,0:T(8,128)S(1)} %bitcast.208, f32[4,6,128]{2,1,0:T(8,128)S(1)} %log_add_fusion, pred[4,1280]{1,0:T(4,128)(4,1)S(1)} %pad_add_fusion, ...), kind=kOutput, calls=%fused_computation.9 | convolution fusion | flops 1045954560 | bytes 32273408 | tf_op jit(solution)/shard_map/while/body/eval_jaxpr/bthd,bkhd->bhtk/dot_general | solution.py:44
  313.8 8.4 multiply_convert_fusion
  326.8 11.1 %convolution_bitcast_fusion = f32[4,1280,6,128]{3,1,2,0:T(8,128)} fusion(bf16[4,128,6,128]{1,3,2,0:T(8,128)(2,1)S(1)} %bitcast.181, f32[4,6,1280,128]{3,2,1,0:T(8,128)} %copy-done.2, f32[4,6,128]{2,1,0:T(8,128)S(1)} %log_add_fusion, pred[4,1280]{1,0:T(4,128)(4,1)S(1)} %pad_add_fusion), kind=kOutput, calls=%fused_computation.19 | convolution fusion | flops 1022361600 | bytes 32261120 | tf_op jit(solution)/shard_map/while/body/eval_jaxpr/bhtk,bthd->bkhd/dot_general | solution.py:56
  337.9 10.4 %slice.43 = f32[4,1024,6,128]{3,1,2,0:T(8,128)} slice(f32[4,1280,6,128]{3,1,2,0:T(8,128)} %convolution_bitcast_fusion), slice={[0:4], [0:1024], [0:6], [0:128]} | slice | bytes 25165824 | tf_op jit(solution)/shard_map/while/body/eval_jaxpr/slice | solution.py:64
  348.3 17.8 %copy.498 = f32[4,1024,6,128]{3,2,1,0:T(8,128)} copy(f32[4,1024,6,128]{3,1,2,0:T(8,128)} %slice.43) | data formatting | bytes 25165824 | tf_op jit(solution)/shard_map/while/body/eval_jaxpr/reshape | solution.py:64
  366.1 16.1 %reshape.404 = f32[32,128,768]{2,1,0:T(8,128)} reshape(f32[4,1024,6,128]{3,2,1,0:T(8,128)} %copy.498) | data formatting | bytes 25165824 | tf_op jit(solution)/shard_map/while/body/eval_jaxpr/reshape | solution.py:64
  386.1 30.2 %scatter_fusion.2 = f32[20,128,768]{2,1,0:T(8,128)} fusion(f32[20,128,768]{2,1,0:T(8,128)} %broadcast.165.clone.1, s32[32]{0:T(128)S(1)} %reshape.345, f32[32,128,768]{2,1,0:T(8,128)} %reshape.404), kind=kCustom, calls=%fused_computation.4 | custom fusion | flops 3145728 | bytes 37748864 | tf_op jit(solution)/shard_map/while/body/eval_jaxpr/scatter-add | solution.py:66
  416.3 6.2 slice.45
  428.1 11.1 %multiply_bitcast_fusion = f32[4,1280,6,128]{3,1,2,0:T(8,128)} fusion(bf16[4,6,128,1280]{2,3,1,0:T(8,128)(2,1)} %fusion, bf16[4,128,6,128]{1,3,2,0:T(8,128)(2,1)} %bitcast.14), kind=kOutput, calls=%fused_computation.16 | convolution fusion | flops 1010565120 | bytes 24379392 | tf_op jit(solution)/shard_map/while/body/eval_jaxpr/bhtk,bthd->bkhd/dot_general | solution.py:53
  439.2 10.4 %slice.40 = f32[4,1024,6,128]{3,1,2,0:T(8,128)} slice(f32[4,1280,6,128]{3,1,2,0:T(8,128)} %multiply_bitcast_fusion), slice={[0:4], [0:1024], [0:6], [0:128]} | slice | bytes 25165824 | tf_op jit(solution)/shard_map/while/body/eval_jaxpr/slice | solution.py:64
  449.6 17.8 %copy.496 = f32[4,1024,6,128]{3,2,1,0:T(8,128)} copy(f32[4,1024,6,128]{3,1,2,0:T(8,128)} %slice.40) | data formatting | bytes 25165824 | tf_op jit(solution)/shard_map/while/body/eval_jaxpr/reshape | solution.py:64
  467.5 16.1 %reshape.402 = f32[32,128,768]{2,1,0:T(8,128)} reshape(f32[4,1024,6,128]{3,2,1,0:T(8,128)} %copy.496) | data formatting | bytes 25165824 | tf_op jit(solution)/shard_map/while/body/eval_jaxpr/reshape | solution.py:64
  487.5 30.1 %scatter_fusion = f32[20,128,768]{2,1,0:T(8,128)} fusion(f32[20,128,768]{2,1,0:T(8,128)} %broadcast.165.clone, s32[32]{0:T(128)S(1)} %reshape.345, f32[32,128,768]{2,1,0:T(8,128)} %reshape.402), kind=kCustom, calls=%fused_computation.2 | custom fusion | flops 3145728 | bytes 37748864 | tf_op jit(solution)/shard_map/while/body/eval_jaxpr/scatter-add | solution.py:66
  517.7 6.0 slice.42
  523.7 43.3 %all-to-all-done.10 = f32[8,256,768]{2,1,0:T(8,128)} async-done(((f32[8,256,768]{2,1,0:T(8,128)}), f32[8,256,768]{2,1,0:T(8,128)}, u32[]{:S(2)}, u32[]{:S(2)}) %all-to-all-start.10) | async-done | bytes 6291488 | tf_op jit(solution)/shard_map/all_to_all | solution.py:239
  583.2 103.5 %pmax.7 = f32[6,256]{1,0:T(8,128)} all-reduce(f32[6,256]{1,0:T(8,128)S(1)} %get-tuple-element.153), channel_id=1, replica_groups=mesh['seq'=8,'head'=4] {'seq'}, use_global_device_ids=true, to_apply=%region_12.13 | all-reduce | flops 1536 | bytes 12288 | tf_op jit(solution)/shard_map/pmax | solution.py:279
  692.2 44.9 %psum.35 = f32[6,256]{1,0:T(8,128)} all-reduce(f32[6,256]{1,0:T(8,128)S(1)} %fusion.9), channel_id=1, replica_groups=mesh['seq'=8,'head'=4] {'seq'}, use_global_device_ids=true, to_apply=%region_15.16 | all-reduce | flops 1536 | bytes 12288 | tf_op jit(solution)/shard_map/psum | solution.py:282
  747.5 32.2 %all-reduce.4.cloned.1.call-done = f32[256,6,128]{2,0,1:T(8,128)} async-done(((f32[256,6,128]{2,0,1:T(8,128)}), f32[256,6,128]{2,0,1:T(8,128)}) %all-reduce.4.cloned.1.call-update) | async-done | bytes 786448 | tf_op jit(solution)/shard_map/psum | solution.py:282
  812.2 9.2 %scatter_fusion.3 = f32[4,128,768]{2,1,0:T(8,128)S(1)} fusion(f32[4,128,768]{2,1,0:T(8,128)S(1)} %slice_add_fusion, s32[16]{0:T(128)S(1)} %copy-done.35, f32[16,128,768]{2,1,0:T(8,128)} %bitcast.47), kind=kCustom, calls=%fused_computation.5 | custom fusion | flops 1572864 | bytes 18874432 | tf_op jit(solution)/shard_map/scatter-add | solution.py:261
  833.5 29.9 %all-reduce.6.cloned.1.call-done = (f32[256,6,128]{2,0,1:T(8,128)}, f32[256,6,128]{2,0,1:T(8,128)}, f32[256,6,128]{0,2,1:T(8,128)}) async-done(((f32[256,6,128]{2,0,1:T(8,128)}, f32[256,6,128]{2,0,1:T(8,128)}, f32[256,6,128]{0,2,1:T(8,128)}), (f32[256,6,128]{2,0,1:T(8,128)}, f32[256,6,128]{2,0,1:T(8,128)}, f32[256,6,128]{0,2,1:T(8,128)})) %all-reduce.6.cloned.1.call-update) | async-done | bytes 2359312 | tf_op jit(solution)/shard_map/psum | solution.py:306
  868.4 9.2 %scatter_fusion.1 = f32[4,128,768]{2,1,0:T(8,128)S(1)} fusion(f32[4,128,768]{2,1,0:T(8,128)S(1)} %slice_add_fusion.1, s32[16]{0:T(128)S(1)} %copy-done.35, f32[16,128,768]{2,1,0:T(8,128)} %bitcast.41), kind=kCustom, calls=%fused_computation.3 | custom fusion | flops 1572864 | bytes 18874432 | tf_op jit(solution)/shard_map/scatter-add | solution.py:256
  (220 shorter events, 191.7 us)
Async XLA Ops:
  7.2 8.0 copy-start.33
  7.2 8.0 copy-start.38
  7.2 8.4 copy-start.26
  9.9 16.0 %all-to-all-start = ((bf16[128,4,768]{2,0,1:T(8,128)(2,1)}), bf16[128,4,768]{2,0,1:T(8,128)(2,1)S(1)}, u32[]{:S(2)}, u32[]{:S(2)}) async-start(bf16[128,4,768]{2,0,1:T(8,128)(2,1)} %copy.369), calls=%async_computation | async-start | bytes 1572864 | tf_op jit(solution)/shard_map/all_to_all | solution.py:90
  26.0 6.1 copy-start.11
  26.0 14.6 %all-to-all-start.2 = ((bf16[128,4,768]{2,0,1:T(8,128)(2,1)}), bf16[128,4,768]{2,0,1:T(8,128)(2,1)}, u32[]{:S(2)}, u32[]{:S(2)}) async-start(bf16[128,4,768]{2,0,1:T(8,128)(2,1)} %copy.382), calls=%async_computation.2 | async-start | bytes 1572864 | tf_op jit(solution)/shard_map/all_to_all | solution.py:89
  30.4 91.1 %copy-start.29 = (pred[8,8,2,4]{1,3,2,0:T(4,128)(4,1)}, pred[8,8,2,4]{1,3,2,0:T(4,128)(4,1)S(1)}, u32[]{:S(2)}) copy-start(pred[8,8,2,4]{1,3,2,0:T(4,128)(4,1)S(1)} %fusion.48) | copy-start | bytes 1540
  40.6 76.5 %all-to-all-start.1 = ((bf16[8,256,768]{2,1,0:T(8,128)(2,1)}), bf16[8,256,768]{2,1,0:T(8,128)(2,1)}, u32[]{:S(2)}, u32[]{:S(2)}) async-start(bf16[8,256,768]{2,1,0:T(8,128)(2,1)} %reshape.323), calls=%async_computation.1 | async-start | bytes 6291456 | tf_op jit(solution)/shard_map/all_to_all | solution.py:183
  50.8 70.0 %copy-start.39 = (s32[256]{0:T(256)S(1)}, s32[256]{0:T(256)}, u32[]{:S(2)}) copy-start(s32[256]{0:T(256)} %param.21) | copy-start | bytes 3076
  117.1 75.1 %all-to-all-start.3 = ((bf16[8,256,768]{2,1,0:T(8,128)(2,1)}), bf16[8,256,768]{2,1,0:T(8,128)(2,1)S(1)}, u32[]{:S(2)}, u32[]{:S(2)}) async-start(bf16[8,256,768]{2,1,0:T(8,128)(2,1)} %reshape.328), calls=%async_computation.3 | async-start | bytes 6291456 | tf_op jit(solution)/shard_map/all_to_all | solution.py:182
  192.2 76.1 %all-to-all-start.4 = ((bf16[128,4,768]{0,2,1:T(8,128)(2,1)}), bf16[128,4,768]{0,2,1:T(8,128)(2,1)}, u32[]{:S(2)}, u32[]{:S(2)}) async-start(bf16[128,4,768]{0,2,1:T(8,128)(2,1)} %bitcast.192), calls=%async_computation.4 | async-start | bytes 1572864 | tf_op jit(solution)/shard_map/all_to_all | solution.py:88
  197.8 8.5 copy-start.15
  225.7 7.5 copy-start.12
  256.8 15.7 %copy-start.25 = (bf16[256,6,128]{2,0,1:T(8,128)(2,1)S(1)}, bf16[256,6,128]{2,0,1:T(8,128)(2,1)}, u32[]{:S(2)}) copy-start(bf16[256,6,128]{2,0,1:T(8,128)(2,1)} %copy.385) | copy-start | bytes 1179652
  268.3 27.9 %all-to-all-start.6 = ((bf16[128,4,768]{0,2,1:T(8,128)(2,1)}), bf16[128,4,768]{0,2,1:T(8,128)(2,1)S(1)}, u32[]{:S(2)}, u32[]{:S(2)}) async-start(bf16[128,4,768]{0,2,1:T(8,128)(2,1)} %bitcast.20), calls=%async_computation.6 | async-start | bytes 1572864 | tf_op jit(solution)/shard_map/all_to_all | solution.py:91
  296.2 26.0 %all-to-all-start.5 = ((bf16[4,128,768]{1,2,0:T(8,128)(2,1)}), bf16[4,128,768]{1,2,0:T(8,128)(2,1)S(1)}, u32[]{:S(2)}, u32[]{:S(2)}) async-start(bf16[4,128,768]{1,2,0:T(8,128)(2,1)} %bitcast.203), calls=%async_computation.5 | async-start | bytes 1572864 | tf_op jit(solution)/shard_map/all_to_all | solution.py:330
  300.8 13.0 %copy-start.23 = (bf16[4,256,6,128]{3,1,2,0:T(8,128)(2,1)S(1)}, bf16[4,256,6,128]{3,1,2,0:T(8,128)(2,1)}, u32[]{:S(2)}) copy-start(bf16[4,256,6,128]{3,1,2,0:T(8,128)(2,1)} %copy-done.22) | copy-start | bytes 4718596
  322.2 15.7 %copy-start.20 = (bf16[4,128,768]{1,2,0:T(8,128)(2,1)}, bf16[4,128,768]{1,2,0:T(8,128)(2,1)S(1)}, u32[]{:S(2)}) copy-start(bf16[4,128,768]{1,2,0:T(8,128)(2,1)S(1)} %all-to-all-done.5) | copy-start | bytes 2359300
  322.2 100.2 %all-to-all-start.7 = ((bf16[4,128,768]{1,2,0:T(8,128)(2,1)}), bf16[4,128,768]{1,2,0:T(8,128)(2,1)S(1)}, u32[]{:S(2)}, u32[]{:S(2)}) async-start(bf16[4,128,768]{1,2,0:T(8,128)(2,1)} %bitcast.202), calls=%async_computation.7 | async-start | bytes 1572864 | tf_op jit(solution)/shard_map/all_to_all | solution.py:331
  423.4 143.7 %all-to-all-start.10 = ((f32[8,256,768]{2,1,0:T(8,128)}), f32[8,256,768]{2,1,0:T(8,128)}, u32[]{:S(2)}, u32[]{:S(2)}) async-start(f32[8,256,768]{2,1,0:T(8,128)} %bitcast.163), calls=%async_computation.10 | async-start | bytes 12582912 | tf_op jit(solution)/shard_map/all_to_all | solution.py:239
  567.1 7.4 copy-start.16
  567.1 7.4 copy-start.37
  567.1 255.4 %all-to-all-start.8 = ((f32[8,256,768]{2,1,0:T(8,128)}), f32[8,256,768]{2,1,0:T(8,128)}, u32[]{:S(2)}, u32[]{:S(2)}) async-start(f32[8,256,768]{2,1,0:T(8,128)} %bitcast.162), calls=%async_computation.8 | async-start | bytes 12582912 | tf_op jit(solution)/shard_map/all_to_all | solution.py:232
  572.0 207.6 %all-reduce.4.cloned.1.call-start = ((), (), s32[]{:S(2)}) async-start(), calls=%async_computation.12 | async-start | bytes 1572864 | tf_op jit(solution)/shard_map/psum | solution.py:282
  572.8 6.0 copy-start.4
  691.2 172.3 %all-reduce.6.cloned.1.call-start = ((), (), s32[]{:S(2)}) async-start(), calls=%async_computation.13 | async-start | bytes 4718592 | tf_op jit(solution)/shard_map/psum | solution.py:306
  802.5 6.5 copy-start.3
  802.5 6.5 copy-start.19
  802.5 6.5 copy-start.32
  822.4 56.1 %all-to-all-start.11 = ((bf16[4,128,768]{2,1,0:T(8,128)(2,1)}), bf16[4,128,768]{2,1,0:T(8,128)(2,1)}, u32[]{:S(2)}, u32[]{:S(2)}) async-start(bf16[4,128,768]{2,1,0:T(8,128)(2,1)} %convert_element_type.127), calls=%async_computation.11 | async-start | bytes 1572864 | tf_op jit(solution)/shard_map/all_to_all | solution.py:333
  878.5 6.9 copy-start.17
  878.5 13.3 %all-to-all-start.9 = ((bf16[4,128,768]{2,1,0:T(8,128)(2,1)}), bf16[4,128,768]{2,1,0:T(8,128)(2,1)S(1)}, u32[]{:S(2)}, u32[]{:S(2)}) async-start(bf16[4,128,768]{2,1,0:T(8,128)(2,1)} %convert_element_type.123), calls=%async_computation.9 | async-start | bytes 1572864 | tf_op jit(solution)/shard_map/all_to_all | solution.py:332
  (22 other events, 76.9 us)
Sparse Core Ops, SparseCore 0:
  691.3 88.3 all-reduce.3
  797.1 66.2 all-reduce.5
where the time goes:
time: 911 us; the launch traced here: 900 us
  waiting for transfers between devices  253 us (28%)
  local copies, waits for them, and re-layouts  228 us (25%)
  blocking collectives  148 us (16%)
  other arithmetic  109 us (12%)
  matrix products  94.3 us (10%)
  starting transfers between devices  53.4 us (6%)
  between operations  14.9 us (2%)
    pmax x1, blocking collectives, body(): lax.pmax(jnp.max(video_scores, axis=-1), 'seq')  104 us
    reshape x4, local copies, waits for them, and re-layouts, spread_grads(): grad_blk[:, :KT * TILE].reshape(block_tiles, KT, TILE, pool_total.shape[2])  67.9 us
    all_to_all x1, waiting for transfers between devices, body(): lax.all_to_all(send_keys, 'seq', split_axis=0, concat_axis=0, tiled=True)  67.4 us
    all_to_all x1, waiting for transfers between devices, body(): lax.all_to_all(send_values, 'seq', split_axis=0, concat_axis=0, tiled=True)  66.3 us
    scatter-add x2, other arithmetic, spread_grads(): pool_total.at[pool_slot].add(tile_part)  60.3 us
    reshape x4, local copies, waits for them, and re-layouts, block_rows(): picked = pool[slot_blk].reshape(block_tiles, KT * TILE, head_count, HD)  46.3 us
    psum x1, blocking collectives, body(): lax.psum((jnp.sum(video_exp, axis=-1), split_product('htk,khd->thd', vide...  44.9 us
    all_to_all x1, waiting for transfers between devices, body(): lax.all_to_all(value_acc[shard_tiles:].reshape(groups, MOST * TILE, featu...  43.3 us
  transfers between devices with their start and end apart: 14, of which 8 were waited for; matrix products, arithmetic and copies ran while one was open for 47% of the time, Pallas kernels for 0%

commit v1 on v0

--- a/solution.py
+++ b/solution.py
@@ -1,3 +1,4 @@
+import functools
 import jax
 import jax.numpy as jnp
 from jax import lax
@@ -10,6 +11,27 @@
 MOST = 2
 NEGATIVE = -1e30
 HIGHEST_PRECISION = lax.Precision.HIGHEST
+
+
+def balance_the_copies(sample, link_axis, d_out, pos_dim):
+    low, wide_out = (lax.axis_size(link_axis), lax.axis_index(link_axis))
+    latest = sample.shape[d_out] // low
+    tile_out = list(sample.shape)
+    tile_out[d_out] = latest
+    k_now = tile_out[pos_dim]
+    tile_out[pos_dim] = k_now * low
+    plain = jnp.zeros(tile_out, sample.dtype)
+    for jj in tuple(range(low)):
+        right_arr = lax.dynamic_slice_in_dim(sample, (wide_out ^ jj) * latest, latest, axis=d_out)
+        if jj:
+            right_arr = lax.ppermute(right_arr, link_axis, [(d, d ^ jj) for d in range(low)])
+        plain = lax.dynamic_update_slice_in_dim(
+            plain, right_arr, (wide_out ^ jj) * k_now, axis=pos_dim
+        )
+    return plain
+
+
+panel_launch = functools.partial(balance_the_copies, link_axis="seq", d_out=0, pos_dim=0)
 
 
 def split_product(form, weights, data):
@@ -180,7 +202,7 @@
     pool_keys, pool_values = build_pool(
         (
             lax.all_to_all(send_keys, "seq", split_axis=0, concat_axis=0, tiled=True),
-            lax.all_to_all(send_values, "seq", split_axis=0, concat_axis=0, tiled=True),
+            panel_launch(send_values),
         )
     )
     start = (

time: 911 us -> 1010 us (1.11)
  local copies, waits for them, and re-layouts: 228 us -> 269 us
  waiting for transfers between devices: 253 us -> 279 us
  starting transfers between devices: 53.4 us -> 69.3 us
    ppermute x0 -> x7, waiting for transfers between devices: none -> 98.7 us  [balance_the_copies(): lax.ppermute(right_arr, link_axis, [(d, d ^ jj) for d in range(low)])]
    all_to_all x1, waiting for transfers between devices: 67.4 us -> 0.01 us  [body(): lax.all_to_all(send_keys, 'seq', split_axis=0, concat_axis=0, tiled=True)]
    reshape x4 -> x6, local copies, waits for them, and re-layouts: 46.3 us -> 67.3 us  [block_rows(): picked = pool[slot_blk].reshape(block_tiles, KT * TILE, head_count, HD)]
    ppermute x0 -> x7, starting transfers between devices: none -> 11.7 us  [balance_the_copies(): lax.ppermute(right_arr, link_axis, [(d, d ^ jj) for d in range(low)])]
    dynamic_update_slice x0 -> x7, local copies, waits for them, and re-layouts: none -> 10.4 us  [balance_the_copies(): lax.dynamic_update_slice_in_dim(plain, right_arr, (wide_out ^ jj) * k_now...]
    unnamed x98 -> x105, local copies, waits for them, and re-layouts: 23.1 us -> 17.2 us
  transfers between devices with their start and end apart: 14 -> 21, of which waited for: 8 -> 10; matrix products, arithmetic and copies ran while one was open for 47% -> 47% of each run, Pallas kernels for 0% -> 0%
where the time goes in v1:
time: 1010 us; the launch traced here: 994 us
  waiting for transfers between devices  279 us (28%)
  local copies, waits for them, and re-layouts  269 us (27%)
  blocking collectives  149 us (15%)
  other arithmetic  112 us (11%)
  matrix products  100 us (10%)
  starting transfers between devices  69.3 us (7%)
  between operations  15 us (1%)
    pmax x1, blocking collectives, body(): lax.pmax(jnp.max(video_scores, axis=-1), 'seq')  104 us
    ppermute x7, waiting for transfers between devices, balance_the_copies(): lax.ppermute(right_arr, link_axis, [(d, d ^ jj) for d in range(low)])  98.7 us
    reshape x4, local copies, waits for them, and re-layouts, spread_grads(): grad_blk[:, :KT * TILE].reshape(block_tiles, KT, TILE, pool_total.shape[2])  67.9 us
    reshape x6, local copies, waits for them, and re-layouts, block_rows(): picked = pool[slot_blk].reshape(block_tiles, KT * TILE, head_count, HD)  67.3 us
    all_to_all x1, waiting for transfers between devices, body(): lax.all_to_all(send_values, 'seq', split_axis=0, concat_axis=0, tiled=True)  64.4 us
    scatter-add x2, other arithmetic, spread_grads(): pool_total.at[pool_slot].add(tile_part)  60.3 us
    psum x1, blocking collectives, body(): lax.psum((jnp.sum(video_exp, axis=-1), split_product('htk,khd->thd', vide...  44.8 us
    all_to_all x1, waiting for transfers between devices, body(): lax.all_to_all(value_acc[shard_tiles:].reshape(groups, MOST * TILE, featu...  43.7 us
  transfers between devices with their start and end apart: 21, of which 10 were waited for; matrix products, arithmetic and copies ran while one was open for 47% of the time, Pallas kernels for 0%

profile of v1, /device:TPU:0, one launch (start us, length us, event | category | flops | bytes accessed | tf_op | source)
XLA Modules:
  0.0 993.9 jit_solution(6511057517692888082)
XLA Ops:
  17.2 8.8 all-to-all-done
  51.9 64.4 %all-to-all-done.5 = bf16[8,256,768]{2,1,0:T(8,128)(2,1)} async-done(((bf16[8,256,768]{2,1,0:T(8,128)(2,1)}), bf16[8,256,768]{2,1,0:T(8,128)(2,1)}, u32[]{:S(2)}, u32[]{:S(2)}) %all-to-all-start.5) | async-done | bytes 3145760 | tf_op jit(solution)/shard_map/all_to_all | solution.py:230
  142.5 47.1 %collective-permute-done.1 = bf16[1,256,768]{2,1,0:T(8,128)(2,1)} collective-permute-done((bf16[1,256,768]{2,1,0:T(8,128)(2,1)}, bf16[1,256,768]{2,1,0:T(8,128)(2,1)}, u32[]{:S(2)}, u32[]{:S(2)}) %collective-permute-start.1) | collective-permute-done | bytes 393248 | tf_op jit(solution)/shard_map/ppermute | solution.py:27
  197.2 37.7 %collective-permute-done.3 = bf16[1,256,768]{2,1,0:T(8,128)(2,1)} collective-permute-done((bf16[1,256,768]{2,1,0:T(8,128)(2,1)}, bf16[1,256,768]{2,1,0:T(8,128)(2,1)}, u32[]{:S(2)}, u32[]{:S(2)}) %collective-permute-start.3) | collective-permute-done | bytes 393248 | tf_op jit(solution)/shard_map/ppermute | solution.py:27
  236.7 13.8 %collective-permute-done.4 = bf16[1,256,768]{2,1,0:T(8,128)(2,1)S(1)} collective-permute-done((bf16[1,256,768]{2,1,0:T(8,128)(2,1)}, bf16[1,256,768]{2,1,0:T(8,128)(2,1)S(1)}, u32[]{:S(2)}, u32[]{:S(2)}) %collective-permute-start.4) | collective-permute-done | bytes 393248 | tf_op jit(solution)/shard_map/ppermute | solution.py:27
  267.4 13.7 %reshape.417 = bf16[4,1024,6,128]{3,2,1,0:T(8,128)(2,1)} reshape(bf16[32,128,768]{2,1,0:T(8,128)(2,1)} %gather_fusion.1) | data formatting | bytes 12582912 | tf_op jit(solution)/shard_map/while/body/eval_jaxpr/reshape | solution.py:197
  281.1 7.5 copy.395
  299.6 13.7 %reshape.416 = bf16[4,1024,6,128]{3,2,1,0:T(8,128)(2,1)} reshape(bf16[32,128,768]{2,1,0:T(8,128)(2,1)} %gather_fusion) | data formatting | bytes 12582912 | tf_op jit(solution)/shard_map/while/body/eval_jaxpr/reshape | solution.py:197
  313.3 11.5 %copy.389 = bf16[4,1024,6,128]{1,3,2,0:T(8,128)(2,1)} copy(bf16[4,1024,6,128]{3,2,1,0:T(8,128)(2,1)} %reshape.416) | data formatting | bytes 12582912 | tf_op jit(solution)/shard_map/while/body/eval_jaxpr/reshape | solution.py:197
  330.5 8.3 bitcast_reduce_fusion
  344.5 10.9 %bitcast_convert_fusion = (bf16[4,128,6,128]{1,3,2,0:T(8,128)(2,1)}, f32[4,6,128,128]{3,2,1,0:T(8,128)}) fusion(f32[4,6,1280,128]{3,2,1,0:T(8,128)} %copy-done.2, f32[4,6,128]{2,1,0:T(8,128)S(1)} %log_add_fusion, pred[4,1280]{1,0:T(4,128)(4,1)S(1)} %pad_add_fusion, bf16[4,256,6,128]{1,3,2,0:T(8,128)(2,1)S(1)} %broadcast_in_dim.186, ...), kind=kOutput, calls=%fused_computation.51 | convolution fusion | flops 1038483456 | bytes 25969664 | tf_op jit(solution)/shard_map/while/body/eval_jaxpr/bhtk,bkhd->bthd/dot_general | solution.py:58
  361.1 13.7 %reshape.418 = bf16[4,1024,6,128]{3,2,1,0:T(8,128)(2,1)} reshape(bf16[32,128,768]{2,1,0:T(8,128)(2,1)} %gather_fusion.2) | data formatting | bytes 12582912 | tf_op jit(solution)/shard_map/while/body/eval_jaxpr/reshape | solution.py:197
  389.5 12.2 %fusion = bf16[4,6,128,1280]{2,3,1,0:T(8,128)(2,1)} fusion(f32[4,6,1280,128]{3,2,1,0:T(8,128)} %copy-done.2, bf16[4,128,6,128]{1,3,2,0:T(8,128)(2,1)S(1)} %bitcast.185, bf16[4,256,6,128]{3,1,2,0:T(8,128)(2,1)} %broadcast_in_dim.186.clone, bf16[4,1024,6,128]{3,1,2,0:T(8,128)(2,1)} %copy.401, f32[4,6,128]{2,1,0:T(8,128)S(1)} %bitcast.215, ...), kind=kOutput, calls=%fused_computation.10 | convolution fusion | flops 1045954560 | bytes 32273408 | tf_op jit(solution)/shard_map/while/body/eval_jaxpr/bthd,bkhd->bhtk/dot_general | solution.py:66
  401.7 8.9 multiply_convert_fusion
  415.2 11.1 %convolution_bitcast_fusion = f32[4,1280,6,128]{3,1,2,0:T(8,128)} fusion(bf16[4,128,6,128]{1,3,2,0:T(8,128)(2,1)S(1)} %bitcast.186, f32[4,6,1280,128]{3,2,1,0:T(8,128)} %copy-done.2, f32[4,6,128]{2,1,0:T(8,128)S(1)} %copy-done.33, pred[4,1280]{1,0:T(4,128)(4,1)S(1)} %pad_add_fusion), kind=kOutput, calls=%fused_computation.20 | convolution fusion | flops 1022361600 | bytes 32261120 | tf_op jit(solution)/shard_map/while/body/eval_jaxpr/bhtk,bthd->bkhd/dot_general | solution.py:78
  426.3 10.3 %slice.45 = f32[4,1024,6,128]{3,1,2,0:T(8,128)} slice(f32[4,1280,6,128]{3,1,2,0:T(8,128)} %convolution_bitcast_fusion), slice={[0:4], [0:1024], [0:6], [0:128]} | slice | bytes 25165824 | tf_op jit(solution)/shard_map/while/body/eval_jaxpr/slice | solution.py:86
  436.6 17.8 %copy.510 = f32[4,1024,6,128]{3,2,1,0:T(8,128)} copy(f32[4,1024,6,128]{3,1,2,0:T(8,128)} %slice.45) | data formatting | bytes 25165824 | tf_op jit(solution)/shard_map/while/body/eval_jaxpr/reshape | solution.py:86
  454.4 16.0 %reshape.421 = f32[32,128,768]{2,1,0:T(8,128)} reshape(f32[4,1024,6,128]{3,2,1,0:T(8,128)} %copy.510) | data formatting | bytes 25165824 | tf_op jit(solution)/shard_map/while/body/eval_jaxpr/reshape | solution.py:86
  474.4 30.3 %scatter_fusion.2 = f32[20,128,768]{2,1,0:T(8,128)} fusion(f32[20,128,768]{2,1,0:T(8,128)} %broadcast.165.clone.1, s32[32]{0:T(128)S(1)} %reshape.351, f32[32,128,768]{2,1,0:T(8,128)} %reshape.421), kind=kCustom, calls=%fused_computation.5 | custom fusion | flops 3145728 | bytes 37748864 | tf_op jit(solution)/shard_map/while/body/eval_jaxpr/scatter-add | solution.py:88
  511.8 9.7 all-to-all-start.10
  521.5 11.0 %multiply_bitcast_fusion = f32[4,1280,6,128]{3,1,2,0:T(8,128)} fusion(bf16[4,6,128,1280]{2,3,1,0:T(8,128)(2,1)} %fusion, bf16[4,128,6,128]{1,3,2,0:T(8,128)(2,1)S(1)} %bitcast.195), kind=kOutput, calls=%fused_computation.17 | convolution fusion | flops 1010565120 | bytes 24379392 | tf_op jit(solution)/shard_map/while/body/eval_jaxpr/bhtk,bthd->bkhd/dot_general | solution.py:75
  532.5 10.4 %slice.42 = f32[4,1024,6,128]{3,1,2,0:T(8,128)} slice(f32[4,1280,6,128]{3,1,2,0:T(8,128)} %multiply_bitcast_fusion), slice={[0:4], [0:1024], [0:6], [0:128]} | slice | bytes 25165824 | tf_op jit(solution)/shard_map/while/body/eval_jaxpr/slice | solution.py:86
  542.8 17.8 %copy.508 = f32[4,1024,6,128]{3,2,1,0:T(8,128)} copy(f32[4,1024,6,128]{3,1,2,0:T(8,128)} %slice.42) | data formatting | bytes 25165824 | tf_op jit(solution)/shard_map/while/body/eval_jaxpr/reshape | solution.py:86
  560.7 16.1 %reshape.419 = f32[32,128,768]{2,1,0:T(8,128)} reshape(f32[4,1024,6,128]{3,2,1,0:T(8,128)} %copy.508) | data formatting | bytes 25165824 | tf_op jit(solution)/shard_map/while/body/eval_jaxpr/reshape | solution.py:86
  580.7 30.0 %scatter_fusion = f32[20,128,768]{2,1,0:T(8,128)} fusion(f32[20,128,768]{2,1,0:T(8,128)} %broadcast.165.clone, s32[32]{0:T(128)S(1)} %reshape.351, f32[32,128,768]{2,1,0:T(8,128)} %reshape.419), kind=kCustom, calls=%fused_computation.3 | custom fusion | flops 3145728 | bytes 37748864 | tf_op jit(solution)/shard_map/while/body/eval_jaxpr/scatter-add | solution.py:88
  616.8 43.7 %all-to-all-done.10 = f32[8,256,768]{2,1,0:T(8,128)} async-done(((f32[8,256,768]{2,1,0:T(8,128)}), f32[8,256,768]{2,1,0:T(8,128)}, u32[]{:S(2)}, u32[]{:S(2)}) %all-to-all-start.10) | async-done | bytes 6291488 | tf_op jit(solution)/shard_map/all_to_all | solution.py:261
  675.8 104.4 %pmax.7 = f32[6,256]{1,0:T(8,128)} all-reduce(f32[6,256]{1,0:T(8,128)S(1)} %get-tuple-element.163), channel_id=1, replica_groups=mesh['seq'=8,'head'=4] {'seq'}, use_global_device_ids=true, to_apply=%region_12.13 | all-reduce | flops 1536 | bytes 12288 | tf_op jit(solution)/shard_map/pmax | solution.py:301
  785.6 44.8 %psum.35 = f32[6,256]{1,0:T(8,128)} all-reduce(f32[6,256]{1,0:T(8,128)S(1)} %fusion.15), channel_id=1, replica_groups=mesh['seq'=8,'head'=4] {'seq'}, use_global_device_ids=true, to_apply=%region_15.16 | all-reduce | flops 1536 | bytes 12288 | tf_op jit(solution)/shard_map/psum | solution.py:304
  840.9 32.2 %all-reduce.4.cloned.1.call-done = f32[256,6,128]{2,0,1:T(8,128)} async-done(((f32[256,6,128]{2,0,1:T(8,128)}), f32[256,6,128]{2,0,1:T(8,128)}) %all-reduce.4.cloned.1.call-update) | async-done | bytes 786448 | tf_op jit(solution)/shard_map/psum | solution.py:304
  905.8 9.2 scatter_fusion.3
  927.0 29.9 %all-reduce.6.cloned.1.call-done = (f32[256,6,128]{2,0,1:T(8,128)}, f32[256,6,128]{2,0,1:T(8,128)}, f32[256,6,128]{0,2,1:T(8,128)}) async-done(((f32[256,6,128]{2,0,1:T(8,128)}, f32[256,6,128]{2,0,1:T(8,128)}, f32[256,6,128]{0,2,1:T(8,128)}), (f32[256,6,128]{2,0,1:T(8,128)}, f32[256,6,128]{2,0,1:T(8,128)}, f32[256,6,128]{0,2,1:T(8,128)})) %all-reduce.6.cloned.1.call-update) | async-done | bytes 2359312 | tf_op jit(solution)/shard_map/psum | solution.py:328
  961.9 9.2 scatter_fusion.1
  (254 shorter events, 252.7 us)
Async XLA Ops:
  9.9 16.0 %all-to-all-start = ((bf16[128,4,768]{2,0,1:T(8,128)(2,1)}), bf16[128,4,768]{2,0,1:T(8,128)(2,1)S(1)}, u32[]{:S(2)}, u32[]{:S(2)}) async-start(bf16[128,4,768]{2,0,1:T(8,128)(2,1)} %copy.378), calls=%async_computation | async-start | bytes 1572864 | tf_op jit(solution)/shard_map/all_to_all | solution.py:112
  26.0 262.6 %copy-start.8 = (bf16[128,4,768]{2,0,1:T(8,128)(2,1)}, bf16[128,4,768]{2,0,1:T(8,128)(2,1)S(1)}, u32[]{:S(2)}) copy-start(bf16[128,4,768]{2,0,1:T(8,128)(2,1)S(1)} %all-to-all-done) | copy-start | bytes 2359300
  26.0 13.8 %all-to-all-start.1 = ((bf16[128,4,768]{2,0,1:T(8,128)(2,1)}), bf16[128,4,768]{2,0,1:T(8,128)(2,1)S(1)}, u32[]{:S(2)}, u32[]{:S(2)}) async-start(bf16[128,4,768]{2,0,1:T(8,128)(2,1)} %copy.391), calls=%async_computation.1 | async-start | bytes 1572864 | tf_op jit(solution)/shard_map/all_to_all | solution.py:111
  29.7 91.9 %copy-start.30 = (pred[8,8,2,4]{1,3,2,0:T(4,128)(4,1)}, pred[8,8,2,4]{1,3,2,0:T(4,128)(4,1)S(1)}, u32[]{:S(2)}) copy-start(pred[8,8,2,4]{1,3,2,0:T(4,128)(4,1)S(1)} %fusion.54) | copy-start | bytes 1540
  39.8 217.8 %copy-start.13 = (bf16[128,4,768]{2,0,1:T(8,128)(2,1)}, bf16[128,4,768]{2,0,1:T(8,128)(2,1)S(1)}, u32[]{:S(2)}) copy-start(bf16[128,4,768]{2,0,1:T(8,128)(2,1)S(1)} %all-to-all-done.1) | copy-start | bytes 2359300
  39.8 76.5 %all-to-all-start.5 = ((bf16[8,256,768]{2,1,0:T(8,128)(2,1)}), bf16[8,256,768]{2,1,0:T(8,128)(2,1)}, u32[]{:S(2)}, u32[]{:S(2)}) async-start(bf16[8,256,768]{2,1,0:T(8,128)(2,1)} %reshape.327), calls=%async_computation.5 | async-start | bytes 6291456 | tf_op jit(solution)/shard_map/all_to_all | solution.py:230
  51.9 68.9 %copy-start.42 = (s32[256]{0:T(256)S(1)}, s32[256]{0:T(256)}, u32[]{:S(2)}) copy-start(s32[256]{0:T(256)} %param.21) | copy-start | bytes 3076
  116.3 135.8 %all-to-all-start.2 = ((bf16[8,256,768]{2,1,0:T(8,128)(2,1)}), bf16[8,256,768]{2,1,0:T(8,128)(2,1)}, u32[]{:S(2)}, u32[]{:S(2)}) async-start(bf16[8,256,768]{2,1,0:T(8,128)(2,1)} %reshape.332), calls=%async_computation.2 | async-start | bytes 6291456 | tf_op jit(solution)/shard_map/all_to_all | solution.py:204
  124.2 10.0 %copy-start.27 = (bf16[256,768]{1,0:T(8,128)(2,1)S(1)}, bf16[256,768]{1,0:T(8,128)(2,1)}, u32[]{:S(2)}) copy-start(bf16[256,768]{1,0:T(8,128)(2,1)} %param.17) | copy-start | bytes 1179652
  127.8 10.9 %collective-permute-start = (bf16[1,256,768]{2,1,0:T(8,128)(2,1)}, bf16[1,256,768]{2,1,0:T(8,128)(2,1)}, u32[]{:S(2)}, u32[]{:S(2)}) collective-permute-start(bf16[1,256,768]{2,1,0:T(8,128)(2,1)} %get-tuple-element.151), channel_id=1, source_target_pairs={{0,4},{4,0},{8,12},{12,8},{16,20},{20,16},{24,28},{28,24},{1,5},{5... | collective-permute-start | bytes 1179656 | tf_op jit(solution)/shard_map/ppermute | solution.py:27
  128.3 67.1 %collective-permute-start.2 = (bf16[1,256,768]{2,1,0:T(8,128)(2,1)}, bf16[1,256,768]{2,1,0:T(8,128)(2,1)}, u32[]{:S(2)}, u32[]{:S(2)}) collective-permute-start(bf16[1,256,768]{2,1,0:T(8,128)(2,1)} %get-tuple-element.149), channel_id=1, source_target_pairs={{0,12},{4,8},{8,4},{12,0},{16,28},{20,24},{24,20},{28,16},{1,13},{... | collective-permute-start | bytes 1179656 | tf_op jit(solution)/shard_map/ppermute | solution.py:27
  130.0 59.5 %collective-permute-start.1 = (bf16[1,256,768]{2,1,0:T(8,128)(2,1)}, bf16[1,256,768]{2,1,0:T(8,128)(2,1)}, u32[]{:S(2)}, u32[]{:S(2)}) collective-permute-start(bf16[1,256,768]{2,1,0:T(8,128)(2,1)} %get-tuple-element.150), channel_id=1, source_target_pairs={{0,8},{4,12},{8,0},{12,4},{16,24},{20,28},{24,16},{28,20},{1,9},{5... | collective-permute-start | bytes 1179656 | tf_op jit(solution)/shard_map/ppermute | solution.py:27
  130.3 104.7 %collective-permute-start.3 = (bf16[1,256,768]{2,1,0:T(8,128)(2,1)}, bf16[1,256,768]{2,1,0:T(8,128)(2,1)}, u32[]{:S(2)}, u32[]{:S(2)}) collective-permute-start(bf16[1,256,768]{2,1,0:T(8,128)(2,1)} %get-tuple-element.148), channel_id=1, source_target_pairs={{0,16},{4,20},{8,24},{12,28},{16,0},{20,4},{24,8},{28,12},{1,17},{... | collective-permute-start | bytes 1179656 | tf_op jit(solution)/shard_map/ppermute | solution.py:27
  133.2 9.2 copy-start.16
  134.3 210.0 %copy-start.19 = (bf16[256,768]{0,1:T(8,128)(2,1)}, bf16[256,768]{0,1:T(8,128)(2,1)S(1)}, u32[]{:S(2)}) copy-start(bf16[256,768]{0,1:T(8,128)(2,1)S(1)} %copy.388) | copy-start | bytes 1179652
  138.0 117.8 %collective-permute-start.6 = (bf16[1,256,768]{2,1,0:T(8,128)(2,1)}, bf16[1,256,768]{2,1,0:T(8,128)(2,1)}, u32[]{:S(2)}, u32[]{:S(2)}) collective-permute-start(bf16[1,256,768]{2,1,0:T(8,128)(2,1)} %get-tuple-element.145), channel_id=1, source_target_pairs={{0,28},{4,24},{8,20},{12,16},{16,12},{20,8},{24,4},{28,0},{1,29},{... | collective-permute-start | bytes 1179656 | tf_op jit(solution)/shard_map/ppermute | solution.py:27
  138.6 111.9 %collective-permute-start.4 = (bf16[1,256,768]{2,1,0:T(8,128)(2,1)}, bf16[1,256,768]{2,1,0:T(8,128)(2,1)S(1)}, u32[]{:S(2)}, u32[]{:S(2)}) collective-permute-start(bf16[1,256,768]{2,1,0:T(8,128)(2,1)} %get-tuple-element.147), channel_id=1, source_target_pairs={{0,20},{4,16},{8,28},{12,24},{16,4},{20,0},{24,12},{28,8},{1,21},{... | collective-permute-start | bytes 1179656 | tf_op jit(solution)/shard_map/ppermute | solution.py:27
  189.6 61.8 %collective-permute-start.5 = (bf16[1,256,768]{2,1,0:T(8,128)(2,1)}, bf16[1,256,768]{2,1,0:T(8,128)(2,1)S(1)}, u32[]{:S(2)}, u32[]{:S(2)}) collective-permute-start(bf16[1,256,768]{2,1,0:T(8,128)(2,1)} %get-tuple-element.146), channel_id=1, source_target_pairs={{0,24},{4,28},{8,16},{12,20},{16,8},{20,12},{24,0},{28,4},{1,25},{... | collective-permute-start | bytes 1179656 | tf_op jit(solution)/shard_map/ppermute | solution.py:27
  252.1 72.7 %all-to-all-start.3 = ((bf16[128,4,768]{0,2,1:T(8,128)(2,1)}), bf16[128,4,768]{0,2,1:T(8,128)(2,1)S(1)}, u32[]{:S(2)}, u32[]{:S(2)}) async-start(bf16[128,4,768]{0,2,1:T(8,128)(2,1)} %bitcast.200), calls=%async_computation.3 | async-start | bytes 1572864 | tf_op jit(solution)/shard_map/all_to_all | solution.py:110
  313.3 15.7 %copy-start.23 = (bf16[256,6,128]{2,0,1:T(8,128)(2,1)S(1)}, bf16[256,6,128]{2,0,1:T(8,128)(2,1)}, u32[]{:S(2)}) copy-start(bf16[256,6,128]{2,0,1:T(8,128)(2,1)} %copy.394) | copy-start | bytes 1179652
  324.8 57.4 %all-to-all-start.6 = ((bf16[128,4,768]{0,2,1:T(8,128)(2,1)}), bf16[128,4,768]{0,2,1:T(8,128)(2,1)S(1)}, u32[]{:S(2)}, u32[]{:S(2)}) async-start(bf16[128,4,768]{0,2,1:T(8,128)(2,1)} %bitcast.21), calls=%async_computation.6 | async-start | bytes 1572864 | tf_op jit(solution)/shard_map/all_to_all | solution.py:113
  344.4 45.1 %copy-start.32 = (f32[4,6,128]{2,1,0:T(8,128)}, f32[4,6,128]{2,1,0:T(8,128)S(1)}, u32[]{:S(2)}) copy-start(f32[4,6,128]{2,1,0:T(8,128)S(1)} %log_add_fusion) | copy-start | bytes 36868
  382.2 28.4 %all-to-all-start.4 = ((bf16[4,128,768]{1,2,0:T(8,128)(2,1)}), bf16[4,128,768]{1,2,0:T(8,128)(2,1)S(1)}, u32[]{:S(2)}, u32[]{:S(2)}) async-start(bf16[4,128,768]{1,2,0:T(8,128)(2,1)} %bitcast.17), calls=%async_computation.4 | async-start | bytes 1572864 | tf_op jit(solution)/shard_map/all_to_all | solution.py:352
  401.7 13.5 %copy-start.33 = (f32[4,6,128]{2,1,0:T(8,128)S(1)}, f32[4,6,128]{2,1,0:T(8,128)}, u32[]{:S(2)}) copy-start(f32[4,6,128]{2,1,0:T(8,128)} %copy-done.32) | copy-start | bytes 36868
  410.6 15.7 %copy-start.21 = (bf16[4,128,768]{1,2,0:T(8,128)(2,1)}, bf16[4,128,768]{1,2,0:T(8,128)(2,1)S(1)}, u32[]{:S(2)}) copy-start(bf16[4,128,768]{1,2,0:T(8,128)(2,1)S(1)} %all-to-all-done.4) | copy-start | bytes 2359300
  410.6 100.3 %all-to-all-start.7 = ((bf16[4,128,768]{1,2,0:T(8,128)(2,1)}), bf16[4,128,768]{1,2,0:T(8,128)(2,1)S(1)}, u32[]{:S(2)}, u32[]{:S(2)}) async-start(bf16[4,128,768]{1,2,0:T(8,128)(2,1)} %bitcast.210), calls=%async_computation.7 | async-start | bytes 1572864 | tf_op jit(solution)/shard_map/all_to_all | solution.py:353
  511.8 148.7 %all-to-all-start.10 = ((f32[8,256,768]{2,1,0:T(8,128)}), f32[8,256,768]{2,1,0:T(8,128)}, u32[]{:S(2)}, u32[]{:S(2)}) async-start(f32[8,256,768]{2,1,0:T(8,128)} %bitcast.166), calls=%async_computation.10 | async-start | bytes 12582912 | tf_op jit(solution)/shard_map/all_to_all | solution.py:261
  660.5 255.5 %all-to-all-start.8 = ((f32[8,256,768]{2,1,0:T(8,128)}), f32[8,256,768]{2,1,0:T(8,128)}, u32[]{:S(2)}, u32[]{:S(2)}) async-start(f32[8,256,768]{2,1,0:T(8,128)} %bitcast.165), calls=%async_computation.8 | async-start | bytes 12582912 | tf_op jit(solution)/shard_map/all_to_all | solution.py:254
  665.5 207.6 %all-reduce.4.cloned.1.call-start = ((), (), s32[]{:S(2)}) async-start(), calls=%async_computation.12 | async-start | bytes 1572864 | tf_op jit(solution)/shard_map/psum | solution.py:304
  784.7 172.3 %all-reduce.6.cloned.1.call-start = ((), (), s32[]{:S(2)}) async-start(), calls=%async_computation.13 | async-start | bytes 4718592 | tf_op jit(solution)/shard_map/psum | solution.py:328
  916.0 56.1 %all-to-all-start.11 = ((bf16[4,128,768]{2,1,0:T(8,128)(2,1)}), bf16[4,128,768]{2,1,0:T(8,128)(2,1)}, u32[]{:S(2)}, u32[]{:S(2)}) async-start(bf16[4,128,768]{2,1,0:T(8,128)(2,1)} %convert_element_type.127), calls=%async_computation.11 | async-start | bytes 1572864 | tf_op jit(solution)/shard_map/all_to_all | solution.py:355
  972.0 13.3 %all-to-all-start.9 = ((bf16[4,128,768]{2,1,0:T(8,128)(2,1)}), bf16[4,128,768]{2,1,0:T(8,128)(2,1)S(1)}, u32[]{:S(2)}, u32[]{:S(2)}) async-start(bf16[4,128,768]{2,1,0:T(8,128)(2,1)} %convert_element_type.123), calls=%async_computation.9 | async-start | bytes 1572864 | tf_op jit(solution)/shard_map/all_to_all | solution.py:354
  (32 other events, 154.9 us)
Sparse Core Ops, SparseCore 0:
  784.8 88.3 all-reduce.3
  890.7 66.2 all-reduce.5
